TPU v7x, 32 devices: a whole 2x2x4 slice. The times are simulated.
32 devices in a mesh: dp: 8 (over z, core), space: 4 (over y, x).
Axes of the slice: x: 2, y: 2, z: 4, core: 2. Of those that a mesh axis runs over, the one named last changes fastest.
Arguments:
- inputs: bfloat16 [8, 24, 32, 32, 256], P('dp', 'space'), may hold values from -6 to 6
- kernels: bfloat16 [2, 3, 3, 256, 256], P(None, None, None, 'dp'), may hold values from -0.125 to 0.125
- cotangent: bfloat16 [8, 24, 32, 32, 256], P('dp', 'space'), may hold values from -0.01171875 to 0.01171875
- adjacency: int32 [24, 4, 3], P('space'), may hold values from 0 to 23, as said below
Outputs:
- final_state: bfloat16 [8, 24, 32, 32, 256], P('dp', 'space')
- kernel_grads: float32 [2, 3, 3, 256, 256], P(None, None, None, 'dp')
Inputs may be any that keep to these rules, and one draw needn't show every extreme that they name: Entry [t, e] = (n, f, r): edge e of tile t meets edge f of tile n, and r = 1 where the two edges are read in opposite directions along the shared line. The relation is symmetric: adjacency[n, f] = (t, e, r). The tiles form 2 x 2 blocks on the six faces of a cube, numbered in an order drawn from the seed.
All inputs are finite; a program needn't handle non-finite values.
Results may differ from a plain program's by a relative error of at most 0.005.
Values may be sent and summed in bfloat16 or wider, within the bound.
A program may use at most 192 MiB of HBM per device.

v0:
```python
import jax
import jax.numpy as jnp
from jax import lax
from jax.sharding import PartitionSpec as P

LAYERS = 2


def edge_strips(tile_field):
    return jnp.stack(
        [
            tile_field[:, :, 0],
            tile_field[:, :, -1],
            tile_field[:, :, :, 0],
            tile_field[:, :, :, -1],
        ],
        axis=2,
    )


def orient(strips, adjacency):
    selected = strips[:, adjacency[:, :, 0], adjacency[:, :, 1]]
    flipped = (adjacency[:, :, 2] == 1)[None, :, :, None, None]
    return jnp.where(flipped, selected[:, :, :, ::-1], selected)


def neighbor_rims(tile_field, adjacency):
    gathered = lax.all_gather(edge_strips(tile_field), "space", axis=1, tiled=True)
    return orient(gathered, adjacency)


def returned_rims(rim_values, adjacency):
    gathered = lax.all_gather(rim_values, "space", axis=1, tiled=True)
    return orient(gathered, adjacency)


def with_rim(tile_field, rim_rows):
    middle = jnp.concatenate(
        [rim_rows[:, :, 2][:, :, :, None], tile_field, rim_rows[:, :, 3][:, :, :, None]], axis=3
    )
    corner = jnp.zeros(tile_field.shape[:2] + (1, tile_field.shape[4]), tile_field.dtype)
    top_row = jnp.concatenate([corner, rim_rows[:, :, 0], corner], axis=2)[:, :, None]
    bottom_row = jnp.concatenate([corner, rim_rows[:, :, 1], corner], axis=2)[:, :, None]
    return jnp.concatenate([top_row, middle, bottom_row], axis=2)


def convolve(padded, kernel):
    extent = padded.shape[2] - 2
    channels = padded.shape[-1]
    summed = jnp.zeros(padded.shape[:2] + (extent, extent, kernel.shape[-1]), jnp.float32)
    for row_off in range(3):
        for col_off in range(3):
            patches = padded[:, :, row_off : row_off + extent, col_off : col_off + extent].reshape(
                -1, channels
            )
            summed = summed + jnp.dot(
                patches, kernel[row_off, col_off], preferred_element_type=jnp.float32
            ).reshape(summed.shape)
    return summed


def weight_grad(padded, flat_grad):
    extent = padded.shape[2] - 2
    channels = padded.shape[-1]
    rows_out = []
    for row_off in range(3):
        row_list = []
        for col_off in range(3):
            patches = padded[:, :, row_off : row_off + extent, col_off : col_off + extent].reshape(
                -1, channels
            )
            row_list.append(
                lax.dot_general(
                    patches, flat_grad, (((0,), (0,)), ((), ())), preferred_element_type=jnp.float32
                )
            )
        rows_out.append(jnp.stack(row_list))
    return jnp.stack(rows_out)


def input_grad(flat_grad, kernel, padded_shape):
    extent = padded_shape[2] - 2
    full = extent + 2
    channels = padded_shape[4]
    grid_grad = flat_grad.reshape(padded_shape[:2] + (extent, extent, flat_grad.shape[-1]))
    widened = jnp.pad(grid_grad, ((0, 0), (0, 0), (2, 2), (2, 2), (0, 0)))
    pad_grad = jnp.zeros(padded_shape, jnp.float32)
    for row_off in range(3):
        for col_off in range(3):
            window = widened[
                :, :, 2 - row_off : 2 - row_off + full, 2 - col_off : 2 - col_off + full
            ].reshape(-1, flat_grad.shape[-1])
            contrib = lax.dot_general(
                window,
                kernel[row_off, col_off],
                (((1,), (1,)), ((), ())),
                preferred_element_type=jnp.float32,
            )
            pad_grad = pad_grad + contrib.reshape(padded_shape[:4] + (channels,))
    return pad_grad


def rim_strips(pad_grad):
    return jnp.stack(
        [
            pad_grad[:, :, 0, 1:-1],
            pad_grad[:, :, -1, 1:-1],
            pad_grad[:, :, 1:-1, 0],
            pad_grad[:, :, 1:-1, -1],
        ],
        axis=2,
    )


def add_rim(interior, returned):
    interior = jnp.concatenate(
        [
            interior[:, :, :1] + returned[:, :, 0][:, :, None],
            interior[:, :, 1:-1],
            interior[:, :, -1:] + returned[:, :, 1][:, :, None],
        ],
        axis=2,
    )
    interior = jnp.concatenate(
        [
            interior[:, :, :, :1] + returned[:, :, 2][:, :, :, None],
            interior[:, :, :, 1:-1],
            interior[:, :, :, -1:] + returned[:, :, 3][:, :, :, None],
        ],
        axis=3,
    )
    return interior


def reduce_grad(partial_value):
    space_total = lax.psum(partial_value, "space")
    return lax.psum_scatter(space_total, "dp", scatter_dimension=2, tiled=True)


def per_device(inputs, kernels, cotangent, adjacency):
    weights = lax.all_gather(kernels, "dp", axis=3, tiled=True)
    current = inputs
    stored = []
    for layer_num in range(LAYERS):
        padded = with_rim(current, neighbor_rims(current, adjacency))
        preact = convolve(padded, weights[layer_num])
        current = (current.astype(jnp.float32) + jax.nn.silu(preact)).astype(jnp.bfloat16)
        stored.append((padded, preact))
    upstream = cotangent.astype(jnp.float32)
    kernel_grads = [None] * LAYERS
    for layer_num in range(LAYERS - 1, -1, -1):
        padded, preact = stored[layer_num]
        logistic = jax.nn.sigmoid(preact)
        pre_grad = (upstream * logistic * (1.0 + preact * (1.0 - logistic))).astype(jnp.bfloat16)
        flat_grad = pre_grad.reshape(-1, pre_grad.shape[-1])
        kernel_grads[layer_num] = reduce_grad(weight_grad(padded, flat_grad))
        if layer_num > 0:
            pad_grad = input_grad(flat_grad, weights[layer_num], padded.shape)
            rim_values = rim_strips(pad_grad).astype(jnp.bfloat16)
            returned = returned_rims(rim_values, adjacency).astype(jnp.float32)
            upstream = add_rim(upstream + pad_grad[:, :, 1:-1, 1:-1], returned)
    return (current, jnp.stack(kernel_grads))


def solution(mesh):
    in_specs = (
        P("dp", "space", None, None, None),
        P(None, None, None, "dp", None),
        P("dp", "space", None, None, None),
        P("space", None, None),
    )
    out_specs = (P("dp", "space", None, None, None), P(None, None, None, "dp", None))
    return jax.shard_map(
        per_device, mesh=mesh, in_specs=in_specs, out_specs=out_specs, check_vma=False
    )
```

profile of v0, /device:TPU:0, one launch (start us, length us, event | category | flops | bytes accessed | tf_op | source)
XLA Modules:
  0.0 505.8 jit_solution(17748328288666397905)
XLA Ops:
  12.9 32.7 %all-gather.5.cloned.1.call-done = bf16[1,24,4,32,256]{4,3,1,2,0:T(8,128)(2,1)} async-done(((bf16[1,6,4,32,256]{4,3,1,2,0:T(8,128)(2,1)}), bf16[1,24,4,32,256]{4,3,1,2,0:T(8,128)(2,1)}) %all-gather.5.cloned.1.call-update) | async-done | bytes 1572880 | tf_op jit(solution)/shard_map/all_gather | solution.py:28
  51.8 5.4 %fusion.38 = (bf16[6,32,32,256]{3,2,1,0:T(8,128)(2,1)}, bf16[6,32,32,256]{3,2,1,0:T(8,128)(2,1)}) fusion(bf16[1,6,32,32,256]{4,3,2,1,0:T(8,128)(2,1)S(1)} %copy-done.4, bf16[1,6,32,1,256]{4,3,2,1,0:T(2,128)(2,1)S(1)} %copy.109, bf16[1,6,32,1,256]{4,3,2,1,0:T(2,128)(2,1)S(1)} %copy.110), kind=kLoop, calls=%fused_computation.68 | loop fusion | flops 12582912 | bytes 9633792 | tf_op jit(solution)/shard_map/dot_general | solution.py:56
  57.2 4.9 maximum_maximum_fusion.1
  65.4 10.3 %slice_bitcast_fusion.9 = (bf16[6,32,32,256]{3,2,1,0:T(8,128)(2,1)}, bf16[6,32,32,256]{3,2,1,0:T(8,128)(2,1)}, bf16[6,32,32,256]{3,2,1,0:T(8,128)(2,1)}, bf16[6,...) fusion(bf16[1,6,33,34,256]{4,3,2,1,0:T(8,128)(2,1)S(1)} %get-tuple-element.31, ...), kind=kLoop, calls=%fused_computation.64 | loop fusion | bytes 37748736 | tf_op jit(solution)/shard_map/dot_general | solution.py:56
  81.7 6.2 %fusion.60 = f32[6,32,32,256]{3,1,0,2:T(8,128)} fusion(bf16[6,32,32,256]{3,2,1,0:T(8,128)(2,1)S(1)} %copy-done.18, bf16[3,3,256,256]{3,2,1,0:T(8,128)(2,1)S(1)} %get-tuple-element.46), kind=kOutput, calls=%fused_computation.93 | convolution fusion | flops 805306368 | bytes 9568256 | tf_op jit(solution)/shard_map/dot_general | solution.py:56
  88.0 6.2 %fusion.62 = f32[6,32,32,256]{3,1,0,2:T(8,128)} fusion(bf16[6,32,32,256]{3,2,1,0:T(8,128)(2,1)S(1)} %copy-done.17, bf16[3,3,256,256]{3,2,1,0:T(8,128)(2,1)S(1)} %get-tuple-element.46), kind=kOutput, calls=%fused_computation.95 | convolution fusion | flops 805306368 | bytes 9568256 | tf_op jit(solution)/shard_map/dot_general | solution.py:56
  94.2 6.3 %fusion.64 = f32[6,32,32,256]{3,1,0,2:T(8,128)} fusion(bf16[6,32,32,256]{3,2,1,0:T(8,128)(2,1)S(1)} %copy-done.16, bf16[3,3,256,256]{3,2,1,0:T(8,128)(2,1)S(1)} %get-tuple-element.46), kind=kOutput, calls=%fused_computation.97 | convolution fusion | flops 805306368 | bytes 9568256 | tf_op jit(solution)/shard_map/dot_general | solution.py:56
  100.5 6.4 %fusion.66 = f32[6,32,32,256]{3,1,0,2:T(8,128)} fusion(bf16[6,32,32,256]{3,2,1,0:T(8,128)(2,1)S(1)} %copy-done.21, bf16[3,3,256,256]{3,2,1,0:T(8,128)(2,1)S(1)} %get-tuple-element.46), kind=kOutput, calls=%fused_computation.99 | convolution fusion | flops 805306368 | bytes 9568256 | tf_op jit(solution)/shard_map/dot_general | solution.py:56
  106.9 6.3 %fusion.68 = f32[6,32,32,256]{3,1,0,2:T(8,128)} fusion(bf16[6,32,32,256]{3,2,1,0:T(8,128)(2,1)S(1)} %bitcast.431, bf16[3,3,256,256]{3,2,1,0:T(8,128)(2,1)S(1)} %get-tuple-element.46), kind=kOutput, calls=%fused_computation.101 | convolution fusion | flops 805306368 | bytes 9568256 | tf_op jit(solution)/shard_map/dot_general | solution.py:56
  113.1 6.2 %fusion.70 = f32[6,32,32,256]{3,1,0,2:T(8,128)} fusion(bf16[6,32,32,256]{3,2,1,0:T(8,128)(2,1)S(1)} %copy-done.19, bf16[3,3,256,256]{3,2,1,0:T(8,128)(2,1)S(1)} %get-tuple-element.46), kind=kOutput, calls=%fused_computation.103 | convolution fusion | flops 805306368 | bytes 9568256 | tf_op jit(solution)/shard_map/dot_general | solution.py:56
  119.4 6.7 %fusion.72 = f32[6,32,32,256]{3,1,0,2:T(8,128)} fusion(bf16[6,32,32,256]{3,2,1,0:T(8,128)(2,1)S(1)} %copy-done.15, bf16[3,3,256,256]{3,2,1,0:T(8,128)(2,1)S(1)} %get-tuple-element.46), kind=kOutput, calls=%fused_computation.105 | convolution fusion | flops 805306368 | bytes 9568256 | tf_op jit(solution)/shard_map/dot_general | solution.py:56
  126.1 6.2 %fusion.74 = f32[6,32,32,256]{3,1,0,2:T(8,128)} fusion(bf16[6,32,32,256]{3,2,1,0:T(8,128)(2,1)S(1)} %copy-done.14, bf16[3,3,256,256]{3,2,1,0:T(8,128)(2,1)S(1)} %get-tuple-element.46), kind=kOutput, calls=%fused_computation.107 | convolution fusion | flops 805306368 | bytes 9568256 | tf_op jit(solution)/shard_map/dot_general | solution.py:56
  132.3 22.0 %fusion.5 = (bf16[1,6,32,32,256]{4,2,1,3,0:T(8,128)(2,1)S(1)}, f32[6,32,32,256]{3,1,0,2:T(8,128)}) fusion(bf16[1,6,32,32,256]{4,3,2,1,0:T(8,128)(2,1)S(1)} %copy-done.5, f32[6,32,32,256]{3,1,0,2:T(8,128)} %fusion.60, f32[6,32,32,256]{3,1,0,2:T(8,128)} %fusion.62, f32[6,32,32,256]{3,1,0,2:T(8,128)} %fusion.64, f32[6,32,32,256]{3,1,0,2:T(8,128)} %fusion.66, ...), kind=kOutput, calls=%fused_computation.15 | convolution fusion | flops 828899328 | bytes 66191360 | tf_op jit(solution)/shard_map/dot_general | solution.py:56
  155.9 4.5 fusion.141
  160.4 25.7 %all-gather.9.cloned.1.call-done = bf16[1,24,4,32,256]{4,3,1,2,0:T(8,128)(2,1)} async-done(((bf16[1,6,4,32,256]{4,3,1,2,0:T(8,128)(2,1)}), bf16[1,24,4,32,256]{4,3,1,2,0:T(8,128)(2,1)}) %all-gather.9.cloned.1.call-update) | async-done | bytes 1572880 | tf_op jit(solution)/shard_map/all_gather | solution.py:28
  214.9 7.1 %slice_bitcast_fusion.3 = (bf16[6,32,32,256]{3,1,0,2:T(8,128)(2,1)}, bf16[6,32,32,256]{3,1,0,2:T(8,128)(2,1)}, bf16[6,32,32,256]{3,1,0,2:T(8,128)(2,1)}) fusion(bf16[1,6,33,34,256]{4,2,1,3,0:T(8,128)(2,1)S(1)} %get-tuple-element.33), kind=kLoop, calls=%fused_computation.54 | loop fusion | bytes 18874368 | tf_op jit(solution)/shard_map/dot_general | solution.py:56
  229.3 21.6 %fusion.1 = (bf16[1,6,32,32,256]{4,2,1,3,0:T(8,128)(2,1)S(1)}, bf16[1,6,32,32,256]{4,2,1,3,0:T(8,128)(2,1)}) fusion(bf16[1,6,32,32,256]{4,3,2,1,0:T(8,128)(2,1)} %param.6, bf16[1,6,32,32,256]{4,2,1,3,0:T(8,128)(2,1)} %copy-done.2, bf16[3,3,256,256]{3,2,1,0:T(8,128)(2,1)} %get-tuple-element.47, bf16[1,6,33,34,256]{4,2,1,3,0:T(8,128)(2,1)S(1)} %get-tuple-element.33, ...), kind=kOutput, calls=%fused_computation.7 | convolution fusion | flops 839909376 | bytes 66191360 | tf_op jit(solution)/shard_map/dot_general | solution.py:56
  258.9 4.3 slice_bitcast_fusion.6
  263.1 4.6 fusion.28
  267.7 4.7 fusion.25
  272.4 4.6 fusion.22
  277.0 4.7 fusion.19
  281.7 4.6 fusion.16
  286.3 4.6 fusion.13
  290.8 4.6 fusion.7
  295.5 4.6 fusion.10
  300.1 27.1 %fusion.164 = (bf16[1,6,34,34,256]{4,2,1,3,0:T(8,128)(2,1)}, f32[1,6,34,34,256]{4,2,1,3,0:T(8,128)}) fusion(bf16[3,3,256,256]{3,2,1,0:T(8,128)(2,1)} %get-tuple-element.47, bf16[1,6,32,32,256]{4,2,1,3,0:T(8,128)(2,1)S(1)} %get-tuple-element.12, f32[6,34,34,256]{3,1,0,2:T(8,128)} %fusion.28, f32[6,34,34,256]{3,1,0,2:T(8,128)} %fusion.25, ...), kind=kOutput, calls=%fused_computation.247 | convolution fusion | flops 925095936 | bytes 80777216 | tf_op jit(solution)/shard_map/dot_general | solution.py:93
  340.1 6.4 %convert_add_fusion = f32[1,6,32,32,256]{4,2,1,3,0:T(8,128)S(1)} fusion(f32[1,6,34,34,256]{4,2,1,3,0:T(8,128)} %get-tuple-element.65, bf16[1,6,32,32,256]{4,3,2,1,0:T(8,128)(2,1)} %param.6), kind=kLoop, calls=%fused_computation.4 | loop fusion | flops 3145728 | bytes 15728640 | tf_op jit(solution)/shard_map/add | solution.py:161
  357.7 13.4 %all-gather.11.cloned.1.call-done = bf16[1,24,4,32,256]{4,3,1,2,0:T(8,128)(2,1)} async-done(((bf16[1,6,4,32,256]{4,3,1,2,0:T(8,128)(2,1)}), bf16[1,24,4,32,256]{4,3,1,2,0:T(8,128)(2,1)}) %all-gather.11.cloned.1.call-update) | async-done | bytes 1572880 | tf_op jit(solution)/shard_map/all_gather | solution.py:33
  405.5 5.4 %reduce-scatter.5.cloned.1.call-done = f32[3,3,32,256]{3,2,1,0:T(8,128)} async-done(((f32[3,3,256,256]{3,2,1,0:T(8,128)}), f32[3,3,32,256]{3,2,1,0:T(8,128)}) %reduce-scatter.5.cloned.1.call-update) | async-done | bytes 294928 | tf_op jit(solution)/shard_map/reduce_scatter | solution.py:137
  410.8 38.1 %reduce-scatter.3.cloned.1.call-done = f32[3,3,32,256]{3,2,1,0:T(8,128)} async-done(((f32[3,3,256,256]{3,2,1,0:T(8,128)}), f32[3,3,32,256]{3,2,1,0:T(8,128)}) %reduce-scatter.3.cloned.1.call-update) | async-done | bytes 294928 | tf_op jit(solution)/shard_map/reduce_scatter | solution.py:137
  452.5 44.4 %all-reduce.4.cloned.1.call-done = (f32[3,3,32,256]{3,2,1,0:T(8,128)}, f32[3,3,32,256]{3,2,1,0:T(8,128)}) async-done(((f32[3,3,32,256]{3,2,1,0:T(8,128)}, f32[3,3,32,256]{3,2,1,0:T(8,128)}), (f32[3,3,32,256]{3,2,1,0:T(8,128)}, f32[3,3,32,256]{3,2,1,0:T(8,128)})) %all-reduce.4.cloned.1.call-update) | async-done | bytes 589840 | tf_op jit(solution)/shard_map/psum | solution.py:136
  (191 shorter events, 129.9 us)
Async XLA Ops:
  7.2 3.9 copy-start.4
  7.2 5.6 %copy-start.40 = (s32[6,4,3]{0,1,2:T(4,128)S(1)}, s32[6,4,3]{0,1,2:T(4,128)}, u32[]{:S(2)}) copy-start(s32[6,4,3]{0,1,2:T(4,128)} %param.7) | copy-start | bytes 868
  7.2 38.5 %all-gather.5.cloned.1.call-start = ((), (), s32[]{:S(2)}) async-start(), calls=%async_computation.2 | async-start | bytes 1966080 | tf_op jit(solution)/shard_map/all_gather | solution.py:28
  11.9 66.8 %all-gather.7.cloned.1.call-start = ((), (), s32[]{:S(2)}) async-start(), calls=%async_computation.3 | async-start | bytes 2654208 | tf_op jit(solution)/shard_map/all_gather | solution.py:141
  12.7 173.4 %all-gather.9.cloned.1.call-start = ((), (), s32[]{:S(2)}) async-start(), calls=%async_computation.4 | async-start | bytes 1966080 | tf_op jit(solution)/shard_map/all_gather | solution.py:28
  81.7 6.2 %copy-start.17 = (bf16[6,32,32,256]{3,2,1,0:T(8,128)(2,1)S(1)}, bf16[6,32,32,256]{3,2,1,0:T(8,128)(2,1)}, u32[]{:S(2)}) copy-start(bf16[6,32,32,256]{3,2,1,0:T(8,128)(2,1)} %get-tuple-element.29) | copy-start | bytes 9437188
  88.0 6.2 %copy-start.16 = (bf16[6,32,32,256]{3,2,1,0:T(8,128)(2,1)S(1)}, bf16[6,32,32,256]{3,2,1,0:T(8,128)(2,1)}, u32[]{:S(2)}) copy-start(bf16[6,32,32,256]{3,2,1,0:T(8,128)(2,1)} %get-tuple-element.27) | copy-start | bytes 9437188
  94.2 6.3 %copy-start.21 = (bf16[6,32,32,256]{3,2,1,0:T(8,128)(2,1)S(1)}, bf16[6,32,32,256]{3,2,1,0:T(8,128)(2,1)}, u32[]{:S(2)}) copy-start(bf16[6,32,32,256]{3,2,1,0:T(8,128)(2,1)} %get-tuple-element.41) | copy-start | bytes 9437188
  106.9 6.3 %copy-start.19 = (bf16[6,32,32,256]{3,2,1,0:T(8,128)(2,1)S(1)}, bf16[6,32,32,256]{3,2,1,0:T(8,128)(2,1)}, u32[]{:S(2)}) copy-start(bf16[6,32,32,256]{3,2,1,0:T(8,128)(2,1)} %get-tuple-element.40) | copy-start | bytes 9437188
  113.1 6.3 %copy-start.15 = (bf16[6,32,32,256]{3,2,1,0:T(8,128)(2,1)S(1)}, bf16[6,32,32,256]{3,2,1,0:T(8,128)(2,1)}, u32[]{:S(2)}) copy-start(bf16[6,32,32,256]{3,2,1,0:T(8,128)(2,1)} %get-tuple-element.67) | copy-start | bytes 9437188
  119.4 6.7 %copy-start.14 = (bf16[6,32,32,256]{3,2,1,0:T(8,128)(2,1)S(1)}, bf16[6,32,32,256]{3,2,1,0:T(8,128)(2,1)}, u32[]{:S(2)}) copy-start(bf16[6,32,32,256]{3,2,1,0:T(8,128)(2,1)} %get-tuple-element.66) | copy-start | bytes 9437188
  126.1 6.2 %copy-start.5 = (bf16[1,6,32,32,256]{4,3,2,1,0:T(8,128)(2,1)S(1)}, bf16[1,6,32,32,256]{4,3,2,1,0:T(8,128)(2,1)}, u32[]{:S(2)}) copy-start(bf16[1,6,32,32,256]{4,3,2,1,0:T(8,128)(2,1)} %param.4) | copy-start | bytes 9437188
  126.1 6.2 %copy-start.12 = (bf16[6,32,32,256]{3,2,1,0:T(8,128)(2,1)S(1)}, bf16[6,32,32,256]{3,2,1,0:T(8,128)(2,1)}, u32[]{:S(2)}) copy-start(bf16[6,32,32,256]{3,2,1,0:T(8,128)(2,1)} %get-tuple-element.68) | copy-start | bytes 9437188
  154.4 48.6 %copy-start.2 = (bf16[1,6,32,32,256]{4,2,1,3,0:T(8,128)(2,1)}, bf16[1,6,32,32,256]{4,2,1,3,0:T(8,128)(2,1)S(1)}, u32[]{:S(2)}) copy-start(bf16[1,6,32,32,256]{4,2,1,3,0:T(8,128)(2,1)S(1)} %get-tuple-element.62) | copy-start | bytes 9437188
  155.9 215.2 %all-gather.11.cloned.1.call-start = ((), (), s32[]{:S(2)}) async-start(), calls=%async_computation.5 | async-start | bytes 1966080 | tf_op jit(solution)/shard_map/all_gather | solution.py:33
  195.4 15.9 %copy-start = (bf16[1,6,33,34,256]{4,2,1,3,0:T(8,128)(2,1)}, bf16[1,6,33,34,256]{4,2,1,3,0:T(8,128)(2,1)S(1)}, u32[]{:S(2)}) copy-start(bf16[1,6,33,34,256]{4,2,1,3,0:T(8,128)(2,1)S(1)} %get-tuple-element.32) | copy-start | bytes 10340356
  203.5 18.5 %copy-start.25 = (bf16[6,32,32,256]{3,1,0,2:T(8,128)(2,1)}, bf16[6,32,32,256]{3,1,0,2:T(8,128)(2,1)S(1)}, u32[]{:S(2)}) copy-start(bf16[6,32,32,256]{3,1,0,2:T(8,128)(2,1)S(1)} %get-tuple-element.35) | copy-start | bytes 9437188
  203.5 22.1 %copy-start.23 = (bf16[6,32,32,256]{3,1,0,2:T(8,128)(2,1)}, bf16[6,32,32,256]{3,1,0,2:T(8,128)(2,1)S(1)}, u32[]{:S(2)}) copy-start(bf16[6,32,32,256]{3,1,0,2:T(8,128)(2,1)S(1)} %get-tuple-element.34) | copy-start | bytes 9437188
  258.9 4.3 copy-start.27
  340.1 70.8 %reduce-scatter.5.cloned.1.call-start = ((), (), s32[]{:S(2)}) async-start(), calls=%async_computation.7 | async-start | bytes 2654208 | tf_op jit(solution)/shard_map/reduce_scatter | solution.py:137
  346.5 4.6 copy-start.11
  346.5 4.6 copy-start.37
  346.5 4.6 copy-start.38
  346.6 4.6 copy-start.39
  346.6 4.6 copy-start.33
  346.6 4.6 copy-start.34
  346.6 4.6 copy-start.35
  357.6 19.9 %slice-start = ((s8[6291456]{0:T(1024)(128)(4,1)}), s8[2097152]{0:T(1024)(128)(4,1)S(1)}, s32[]{:S(2)}) async-start(s8[6291456]{0:T(1024)(128)(4,1)} %bitcast.433), calls=%async_computation.9 | async-start | bytes 4194304
  357.6 91.3 %reduce-scatter.3.cloned.1.call-start = ((), (), s32[]{:S(2)}) async-start(), calls=%async_computation.6 | async-start | bytes 2654208 | tf_op jit(solution)/shard_map/reduce_scatter | solution.py:137
  373.6 3.9 slice-start.1
  403.8 45.1 %copy-start.13 = (bf16[1,6,32,32,256]{4,2,1,3,0:T(8,128)(2,1)S(1)}, bf16[1,6,32,32,256]{4,2,1,3,0:T(8,128)(2,1)}, u32[]{:S(2)}) copy-start(bf16[1,6,32,32,256]{4,2,1,3,0:T(8,128)(2,1)} %get-tuple-element.13) | copy-start | bytes 9437188
  405.4 91.5 %all-reduce.4.cloned.1.call-start = ((), (), s32[]{:S(2)}) async-start(), calls=%async_computation.8 | async-start | bytes 1179648 | tf_op jit(solution)/shard_map/psum | solution.py:136
  (20 other events, 49.2 us)
Sparse Core Ops, SparseCore 0:
  12.0 33.5 all-gather.4
  47.2 31.4 all-gather.6
  156.0 30.0 all-gather.8
  340.2 30.8 all-gather.10
  373.8 36.9 reduce-scatter.4
  413.0 35.8 reduce-scatter.2
  451.9 44.9 all-reduce.3
where the time goes:
time: 513 us; the launch traced here: 506 us
  matrix products  228 us (44%)
  waiting for transfers between devices  163 us (32%)
  local copies, waits for them, and re-layouts  60.5 us (12%)
  other arithmetic  38.2 us (7%)
  between operations  15.1 us (3%)
    dot_general x18, matrix products, convolve(): jnp.dot(patches, kernel[row_off, col_off], preferred_element_type=jnp.flo...  125 us
    dot_general x9, matrix products, input_grad(): lax.dot_general(window, kernel[row_off, col_off], (((1,), (1,)), ((), ())...  64 us
    all_gather x2, waiting for transfers between devices, neighbor_rims(): lax.all_gather(edge_strips(tile_field), 'space', axis=1, tiled=True)  58.4 us
    psum x1, waiting for transfers between devices, reduce_grad(): space_total = lax.psum(partial_value, 'space')  44.4 us
    reduce_scatter x2, waiting for transfers between devices, reduce_grad(): return lax.psum_scatter(space_total, 'dp', scatter_dimension=2, tiled=True)  43.4 us
    dot_general x18, matrix products, weight_grad(): lax.dot_general(patches, flat_grad, (((0,), (0,)), ((), ())), preferred_e...  39.5 us
    dot_general x3, local copies, waits for them, and re-layouts, convolve(): jnp.dot(patches, kernel[row_off, col_off], preferred_element_type=jnp.flo...  21.7 us
    unnamed x97, local copies, waits for them, and re-layouts  15.4 us
  transfers between devices with their start and end apart: 7, of which 7 were waited for; matrix products, arithmetic and copies ran while one was open for 16% of the time, Pallas kernels for 0%

commit v1 on v0

--- a/solution.py
+++ b/solution.py
@@ -133,7 +133,11 @@
 
 
 def reduce_grad(partial_value):
-    space_total = lax.psum(partial_value, "space")
+    space_total = partial_value
+    for hop in (1, 2):
+        space_total = space_total + lax.ppermute(
+            space_total, "space", [(dev, dev ^ hop) for dev in range(4)]
+        )
     return lax.psum_scatter(space_total, "dp", scatter_dimension=2, tiled=True)
 
 

time: 513 us -> 590 us (1.15)
  waiting for transfers between devices: 163 us -> 222 us
  other arithmetic: 38.2 us -> 46.7 us
    ppermute x0 -> x4, waiting for transfers between devices: none -> 102 us  [reduce_grad(): lax.ppermute(space_total, 'space', [(dev, dev ^ hop) for dev in range(4)])]
    psum x1 -> x0, waiting for transfers between devices: 44.4 us -> none  [reduce_grad(): space_total = lax.psum(partial_value, 'space')]
    all_gather x1, waiting for transfers between devices: 13.4 us -> 25.3 us  [returned_rims(): gathered = lax.all_gather(rim_values, 'space', axis=1, tiled=True)]
    reduce_scatter x2, waiting for transfers between devices: 43.4 us -> 32.7 us  [reduce_grad(): return lax.psum_scatter(space_total, 'dp', scatter_dimension=2, tiled=True)]
    add x0 -> x4, other arithmetic: none -> 8.53 us  [reduce_grad(): space_total + lax.ppermute(space_total, 'space', [(dev, dev ^ hop) for de...]
    unnamed x97 -> x107, local copies, waits for them, and re-layouts: 15.4 us -> 18.9 us
  transfers between devices with their start and end apart: 7 -> 10, of which waited for: 7 -> 8; matrix products, arithmetic and copies ran while one was open for 16% -> 16% of each run, Pallas kernels for 0% -> 0%
where the time goes in v1:
time: 590 us; the launch traced here: 582 us
  matrix products  228 us (39%)
  waiting for transfers between devices  222 us (38%)
  local copies, waits for them, and re-layouts  65.5 us (11%)
  other arithmetic  46.7 us (8%)
  between operations  15.1 us (3%)
    dot_general x18, matrix products, convolve(): jnp.dot(patches, kernel[row_off, col_off], preferred_element_type=jnp.flo...  125 us
    ppermute x4, waiting for transfers between devices, reduce_grad(): lax.ppermute(space_total, 'space', [(dev, dev ^ hop) for dev in range(4)])  102 us
    dot_general x9, matrix products, input_grad(): lax.dot_general(window, kernel[row_off, col_off], (((1,), (1,)), ((), ())...  64 us
    all_gather x2, waiting for transfers between devices, neighbor_rims(): lax.all_gather(edge_strips(tile_field), 'space', axis=1, tiled=True)  58.4 us
    dot_general x18, matrix products, weight_grad(): lax.dot_general(patches, flat_grad, (((0,), (0,)), ((), ())), preferred_e...  39.8 us
    reduce_scatter x2, waiting for transfers between devices, reduce_grad(): return lax.psum_scatter(space_total, 'dp', scatter_dimension=2, tiled=True)  32.7 us
    all_gather x1, waiting for transfers between devices, returned_rims(): gathered = lax.all_gather(rim_values, 'space', axis=1, tiled=True)  25.3 us
    dot_general x3, local copies, waits for them, and re-layouts, convolve(): jnp.dot(patches, kernel[row_off, col_off], preferred_element_type=jnp.flo...  21.7 us
  transfers between devices with their start and end apart: 10, of which 8 were waited for; matrix products, arithmetic and copies ran while one was open for 16% of the time, Pallas kernels for 0%

profile of v1, /device:TPU:0, one launch (start us, length us, event | category | flops | bytes accessed | tf_op | source)
XLA Modules:
  0.0 582.1 jit_solution(11134551720117653302)
XLA Ops:
  12.9 32.7 %all-gather.5.cloned.1.call-done = bf16[1,24,4,32,256]{4,3,1,2,0:T(8,128)(2,1)} async-done(((bf16[1,6,4,32,256]{4,3,1,2,0:T(8,128)(2,1)}), bf16[1,24,4,32,256]{4,3,1,2,0:T(8,128)(2,1)}) %all-gather.5.cloned.1.call-update) | async-done | bytes 1572880 | tf_op jit(solution)/shard_map/all_gather | solution.py:28
  51.8 5.4 fusion.38
  57.2 4.9 maximum_maximum_fusion.1
  65.4 10.3 %slice_bitcast_fusion.9 = (bf16[6,32,32,256]{3,2,1,0:T(8,128)(2,1)}, bf16[6,32,32,256]{3,2,1,0:T(8,128)(2,1)}, bf16[6,32,32,256]{3,2,1,0:T(8,128)(2,1)}, bf16[6,...) fusion(bf16[1,6,33,34,256]{4,3,2,1,0:T(8,128)(2,1)S(1)} %get-tuple-element.29, ...), kind=kLoop, calls=%fused_computation.64 | loop fusion | bytes 37748736 | tf_op jit(solution)/shard_map/dot_general | solution.py:56
  81.7 6.2 %fusion.60 = f32[6,32,32,256]{3,1,0,2:T(8,128)} fusion(bf16[6,32,32,256]{3,2,1,0:T(8,128)(2,1)S(1)} %copy-done.27, bf16[3,3,256,256]{3,2,1,0:T(8,128)(2,1)S(1)} %get-tuple-element.44), kind=kOutput, calls=%fused_computation.93 | convolution fusion | flops 805306368 | bytes 9568256 | tf_op jit(solution)/shard_map/dot_general | solution.py:56
  87.9 6.2 %fusion.62 = f32[6,32,32,256]{3,1,0,2:T(8,128)} fusion(bf16[6,32,32,256]{3,2,1,0:T(8,128)(2,1)S(1)} %copy-done.26, bf16[3,3,256,256]{3,2,1,0:T(8,128)(2,1)S(1)} %get-tuple-element.44), kind=kOutput, calls=%fused_computation.95 | convolution fusion | flops 805306368 | bytes 9568256 | tf_op jit(solution)/shard_map/dot_general | solution.py:56
  94.1 6.3 %fusion.64 = f32[6,32,32,256]{3,1,0,2:T(8,128)} fusion(bf16[6,32,32,256]{3,2,1,0:T(8,128)(2,1)S(1)} %copy-done.25, bf16[3,3,256,256]{3,2,1,0:T(8,128)(2,1)S(1)} %get-tuple-element.44), kind=kOutput, calls=%fused_computation.97 | convolution fusion | flops 805306368 | bytes 9568256 | tf_op jit(solution)/shard_map/dot_general | solution.py:56
  100.4 6.4 %fusion.66 = f32[6,32,32,256]{3,1,0,2:T(8,128)} fusion(bf16[6,32,32,256]{3,2,1,0:T(8,128)(2,1)S(1)} %copy-done.30, bf16[3,3,256,256]{3,2,1,0:T(8,128)(2,1)S(1)} %get-tuple-element.44), kind=kOutput, calls=%fused_computation.99 | convolution fusion | flops 805306368 | bytes 9568256 | tf_op jit(solution)/shard_map/dot_general | solution.py:56
  106.8 6.2 %fusion.68 = f32[6,32,32,256]{3,1,0,2:T(8,128)} fusion(bf16[6,32,32,256]{3,2,1,0:T(8,128)(2,1)S(1)} %bitcast.431, bf16[3,3,256,256]{3,2,1,0:T(8,128)(2,1)S(1)} %get-tuple-element.44), kind=kOutput, calls=%fused_computation.101 | convolution fusion | flops 805306368 | bytes 9568256 | tf_op jit(solution)/shard_map/dot_general | solution.py:56
  113.1 6.2 %fusion.70 = f32[6,32,32,256]{3,1,0,2:T(8,128)} fusion(bf16[6,32,32,256]{3,2,1,0:T(8,128)(2,1)S(1)} %copy-done.28, bf16[3,3,256,256]{3,2,1,0:T(8,128)(2,1)S(1)} %get-tuple-element.44), kind=kOutput, calls=%fused_computation.103 | convolution fusion | flops 805306368 | bytes 9568256 | tf_op jit(solution)/shard_map/dot_general | solution.py:56
  119.3 6.7 %fusion.72 = f32[6,32,32,256]{3,1,0,2:T(8,128)} fusion(bf16[6,32,32,256]{3,2,1,0:T(8,128)(2,1)S(1)} %copy-done.24, bf16[3,3,256,256]{3,2,1,0:T(8,128)(2,1)S(1)} %get-tuple-element.44), kind=kOutput, calls=%fused_computation.105 | convolution fusion | flops 805306368 | bytes 9568256 | tf_op jit(solution)/shard_map/dot_general | solution.py:56
  126.0 6.2 %fusion.74 = f32[6,32,32,256]{3,1,0,2:T(8,128)} fusion(bf16[6,32,32,256]{3,2,1,0:T(8,128)(2,1)S(1)} %copy-done.23, bf16[3,3,256,256]{3,2,1,0:T(8,128)(2,1)S(1)} %get-tuple-element.44), kind=kOutput, calls=%fused_computation.107 | convolution fusion | flops 805306368 | bytes 9568256 | tf_op jit(solution)/shard_map/dot_general | solution.py:56
  132.2 22.0 %fusion.5 = (bf16[1,6,32,32,256]{4,2,1,3,0:T(8,128)(2,1)S(1)}, f32[6,32,32,256]{3,1,0,2:T(8,128)}) fusion(bf16[1,6,32,32,256]{4,3,2,1,0:T(8,128)(2,1)S(1)} %copy-done.5, f32[6,32,32,256]{3,1,0,2:T(8,128)} %fusion.60, f32[6,32,32,256]{3,1,0,2:T(8,128)} %fusion.62, f32[6,32,32,256]{3,1,0,2:T(8,128)} %fusion.64, f32[6,32,32,256]{3,1,0,2:T(8,128)} %fusion.66, ...), kind=kOutput, calls=%fused_computation.15 | convolution fusion | flops 828899328 | bytes 66191360 | tf_op jit(solution)/shard_map/dot_general | solution.py:56
  155.8 4.5 fusion.141
  160.3 25.7 %all-gather.9.cloned.1.call-done = bf16[1,24,4,32,256]{4,3,1,2,0:T(8,128)(2,1)} async-done(((bf16[1,6,4,32,256]{4,3,1,2,0:T(8,128)(2,1)}), bf16[1,24,4,32,256]{4,3,1,2,0:T(8,128)(2,1)}) %all-gather.9.cloned.1.call-update) | async-done | bytes 1572880 | tf_op jit(solution)/shard_map/all_gather | solution.py:28
  214.7 7.1 %slice_bitcast_fusion.3 = (bf16[6,32,32,256]{3,1,0,2:T(8,128)(2,1)}, bf16[6,32,32,256]{3,1,0,2:T(8,128)(2,1)}, bf16[6,32,32,256]{3,1,0,2:T(8,128)(2,1)}) fusion(bf16[1,6,33,34,256]{4,2,1,3,0:T(8,128)(2,1)S(1)} %get-tuple-element.31), kind=kLoop, calls=%fused_computation.54 | loop fusion | bytes 18874368 | tf_op jit(solution)/shard_map/dot_general | solution.py:56
  229.0 21.6 %fusion.1 = (bf16[1,6,32,32,256]{4,2,1,3,0:T(8,128)(2,1)S(1)}, bf16[1,6,32,32,256]{4,2,1,3,0:T(8,128)(2,1)}) fusion(bf16[1,6,32,32,256]{4,3,2,1,0:T(8,128)(2,1)} %param.6, bf16[1,6,32,32,256]{4,2,1,3,0:T(8,128)(2,1)} %copy-done.2, bf16[3,3,256,256]{3,2,1,0:T(8,128)(2,1)} %get-tuple-element.45, bf16[1,6,33,34,256]{4,2,1,3,0:T(8,128)(2,1)S(1)} %get-tuple-element.31, ...), kind=kOutput, calls=%fused_computation.7 | convolution fusion | flops 839909376 | bytes 66191360 | tf_op jit(solution)/shard_map/dot_general | solution.py:56
  262.8 4.5 fusion.28
  267.4 4.7 fusion.25
  272.1 4.7 fusion.22
  276.7 4.7 fusion.19
  281.4 4.6 fusion.16
  286.0 4.6 fusion.13
  290.6 4.6 fusion.7
  295.2 4.6 fusion.10
  299.8 27.0 %fusion.166 = (bf16[1,6,34,34,256]{4,2,1,3,0:T(8,128)(2,1)}, f32[1,6,34,34,256]{4,2,1,3,0:T(8,128)}) fusion(bf16[3,3,256,256]{3,2,1,0:T(8,128)(2,1)} %get-tuple-element.45, bf16[1,6,32,32,256]{4,2,1,3,0:T(8,128)(2,1)S(1)} %get-tuple-element.10, f32[6,34,34,256]{3,1,0,2:T(8,128)} %fusion.28, f32[6,34,34,256]{3,1,0,2:T(8,128)} %fusion.25, ...), kind=kOutput, calls=%fused_computation.249 | convolution fusion | flops 925095936 | bytes 80777216 | tf_op jit(solution)/shard_map/dot_general | solution.py:93
  357.9 25.3 %all-gather.11.cloned.1.call-done = bf16[1,24,4,32,256]{4,3,1,2,0:T(8,128)(2,1)} async-done(((bf16[1,6,4,32,256]{4,3,1,2,0:T(8,128)(2,1)}), bf16[1,24,4,32,256]{4,3,1,2,0:T(8,128)(2,1)}) %all-gather.11.cloned.1.call-update) | async-done | bytes 1572880 | tf_op jit(solution)/shard_map/all_gather | solution.py:33
  426.0 44.4 %collective-permute-done.3 = f32[3,3,256,256]{3,2,1,0:T(8,128)S(1)} collective-permute-done((f32[3,3,256,256]{3,2,1,0:T(8,128)S(1)}, f32[3,3,256,256]{3,2,1,0:T(8,128)S(1)}, u32[]{:S(2)}, u32[]{:S(2)}) %collective-permute-start.3) | collective-permute-done | bytes 2359328 | tf_op jit(solution)/shard_map/ppermute | solution.py:138
  472.6 5.9 %collective-permute-done = f32[3,3,256,256]{3,2,1,0:T(8,128)} collective-permute-done((f32[3,3,256,256]{3,2,1,0:T(8,128)}, f32[3,3,256,256]{3,2,1,0:T(8,128)}, u32[]{:S(2)}, u32[]{:S(2)}) %collective-permute-start) | collective-permute-done | bytes 2359328 | tf_op jit(solution)/shard_map/ppermute | solution.py:138
  481.3 51.2 %collective-permute-done.1 = f32[3,3,256,256]{3,2,1,0:T(8,128)S(1)} collective-permute-done((f32[3,3,256,256]{3,2,1,0:T(8,128)S(1)}, f32[3,3,256,256]{3,2,1,0:T(8,128)S(1)}, u32[]{:S(2)}, u32[]{:S(2)}) %collective-permute-start.1) | collective-permute-done | bytes 2359328 | tf_op jit(solution)/shard_map/ppermute | solution.py:138
  532.5 4.4 fusion.171
  540.4 32.7 %reduce-scatter.3.cloned.1.call-done = f32[3,3,32,256]{3,2,1,0:T(8,128)} async-done(((f32[3,3,256,256]{3,2,1,0:T(8,128)}), f32[3,3,32,256]{3,2,1,0:T(8,128)}) %reduce-scatter.3.cloned.1.call-update) | async-done | bytes 294928 | tf_op jit(solution)/shard_map/reduce_scatter | solution.py:141
  (210 shorter events, 154.3 us)
Async XLA Ops:
  7.2 5.6 copy-start.45
  7.2 38.5 %all-gather.5.cloned.1.call-start = ((), (), s32[]{:S(2)}) async-start(), calls=%async_computation.2 | async-start | bytes 1966080 | tf_op jit(solution)/shard_map/all_gather | solution.py:28
  11.9 66.8 %all-gather.7.cloned.1.call-start = ((), (), s32[]{:S(2)}) async-start(), calls=%async_computation.3 | async-start | bytes 2654208 | tf_op jit(solution)/shard_map/all_gather | solution.py:145
  12.7 173.3 %all-gather.9.cloned.1.call-start = ((), (), s32[]{:S(2)}) async-start(), calls=%async_computation.4 | async-start | bytes 1966080 | tf_op jit(solution)/shard_map/all_gather | solution.py:28
  81.7 6.2 %copy-start.26 = (bf16[6,32,32,256]{3,2,1,0:T(8,128)(2,1)S(1)}, bf16[6,32,32,256]{3,2,1,0:T(8,128)(2,1)}, u32[]{:S(2)}) copy-start(bf16[6,32,32,256]{3,2,1,0:T(8,128)(2,1)} %get-tuple-element.27) | copy-start | bytes 9437188
  87.9 6.2 %copy-start.25 = (bf16[6,32,32,256]{3,2,1,0:T(8,128)(2,1)S(1)}, bf16[6,32,32,256]{3,2,1,0:T(8,128)(2,1)}, u32[]{:S(2)}) copy-start(bf16[6,32,32,256]{3,2,1,0:T(8,128)(2,1)} %get-tuple-element.25) | copy-start | bytes 9437188
  94.1 6.3 %copy-start.30 = (bf16[6,32,32,256]{3,2,1,0:T(8,128)(2,1)S(1)}, bf16[6,32,32,256]{3,2,1,0:T(8,128)(2,1)}, u32[]{:S(2)}) copy-start(bf16[6,32,32,256]{3,2,1,0:T(8,128)(2,1)} %get-tuple-element.39) | copy-start | bytes 9437188
  106.8 6.3 %copy-start.28 = (bf16[6,32,32,256]{3,2,1,0:T(8,128)(2,1)S(1)}, bf16[6,32,32,256]{3,2,1,0:T(8,128)(2,1)}, u32[]{:S(2)}) copy-start(bf16[6,32,32,256]{3,2,1,0:T(8,128)(2,1)} %get-tuple-element.38) | copy-start | bytes 9437188
  113.1 6.2 %copy-start.24 = (bf16[6,32,32,256]{3,2,1,0:T(8,128)(2,1)S(1)}, bf16[6,32,32,256]{3,2,1,0:T(8,128)(2,1)}, u32[]{:S(2)}) copy-start(bf16[6,32,32,256]{3,2,1,0:T(8,128)(2,1)} %get-tuple-element.65) | copy-start | bytes 9437188
  119.3 6.7 %copy-start.23 = (bf16[6,32,32,256]{3,2,1,0:T(8,128)(2,1)S(1)}, bf16[6,32,32,256]{3,2,1,0:T(8,128)(2,1)}, u32[]{:S(2)}) copy-start(bf16[6,32,32,256]{3,2,1,0:T(8,128)(2,1)} %get-tuple-element.64) | copy-start | bytes 9437188
  126.0 6.2 %copy-start.5 = (bf16[1,6,32,32,256]{4,3,2,1,0:T(8,128)(2,1)S(1)}, bf16[1,6,32,32,256]{4,3,2,1,0:T(8,128)(2,1)}, u32[]{:S(2)}) copy-start(bf16[1,6,32,32,256]{4,3,2,1,0:T(8,128)(2,1)} %param.4) | copy-start | bytes 9437188
  126.0 6.2 %copy-start.13 = (bf16[6,32,32,256]{3,2,1,0:T(8,128)(2,1)S(1)}, bf16[6,32,32,256]{3,2,1,0:T(8,128)(2,1)}, u32[]{:S(2)}) copy-start(bf16[6,32,32,256]{3,2,1,0:T(8,128)(2,1)} %get-tuple-element.66) | copy-start | bytes 9437188
  154.2 48.5 %copy-start.2 = (bf16[1,6,32,32,256]{4,2,1,3,0:T(8,128)(2,1)}, bf16[1,6,32,32,256]{4,2,1,3,0:T(8,128)(2,1)S(1)}, u32[]{:S(2)}) copy-start(bf16[1,6,32,32,256]{4,2,1,3,0:T(8,128)(2,1)S(1)} %get-tuple-element.60) | copy-start | bytes 9437188
  155.7 227.4 %all-gather.11.cloned.1.call-start = ((), (), s32[]{:S(2)}) async-start(), calls=%async_computation.5 | async-start | bytes 1966080 | tf_op jit(solution)/shard_map/all_gather | solution.py:33
  195.2 15.8 %copy-start = (bf16[1,6,33,34,256]{4,2,1,3,0:T(8,128)(2,1)}, bf16[1,6,33,34,256]{4,2,1,3,0:T(8,128)(2,1)S(1)}, u32[]{:S(2)}) copy-start(bf16[1,6,33,34,256]{4,2,1,3,0:T(8,128)(2,1)S(1)} %get-tuple-element.30) | copy-start | bytes 10340356
  203.3 18.5 %copy-start.34 = (bf16[6,32,32,256]{3,1,0,2:T(8,128)(2,1)}, bf16[6,32,32,256]{3,1,0,2:T(8,128)(2,1)S(1)}, u32[]{:S(2)}) copy-start(bf16[6,32,32,256]{3,1,0,2:T(8,128)(2,1)S(1)} %get-tuple-element.33) | copy-start | bytes 9437188
  203.3 22.0 %copy-start.32 = (bf16[6,32,32,256]{3,1,0,2:T(8,128)(2,1)}, bf16[6,32,32,256]{3,1,0,2:T(8,128)(2,1)S(1)}, u32[]{:S(2)}) copy-start(bf16[6,32,32,256]{3,1,0,2:T(8,128)(2,1)S(1)} %get-tuple-element.32) | copy-start | bytes 9437188
  339.7 200.7 %reduce-scatter.5.cloned.1.call-start = ((), (), s32[]{:S(2)}) async-start(), calls=%async_computation.7 | async-start | bytes 2654208 | tf_op jit(solution)/shard_map/reduce_scatter | solution.py:141
  341.1 4.9 copy-start.16
  342.6 6.5 %slice-start = ((s8[8355840]{0:T(1024)(128)(4,1)}), s8[4194304]{0:T(1024)(128)(4,1)S(1)}, s32[]{:S(2)}) async-start(s8[8355840]{0:T(1024)(128)(4,1)} %bitcast.433), calls=%async_computation.8 | async-start | bytes 8388608
  344.8 4.4 slice-start.1
  347.6 68.4 %collective-permute-start.2 = (f32[3,3,256,256]{3,2,1,0:T(8,128)}, f32[3,3,256,256]{3,2,1,0:T(8,128)S(1)}, u32[]{:S(2)}, u32[]{:S(2)}) collective-permute-start(f32[3,3,256,256]{3,2,1,0:T(8,128)} %pad_maximum_fusion.8), channel_id=1, source_target_pairs={{0,1},{1,0},{2,3},{3,2},{4,5},{5,4},{6,7},{7,6},{8,9},{9,8},{10,11... | collective-permute-start | bytes 7077896 | tf_op jit(solution)/shard_map/ppermute | solution.py:138
  391.4 5.1 slice-start.2
  417.5 53.0 %collective-permute-start.3 = (f32[3,3,256,256]{3,2,1,0:T(8,128)S(1)}, f32[3,3,256,256]{3,2,1,0:T(8,128)S(1)}, u32[]{:S(2)}, u32[]{:S(2)}) collective-permute-start(f32[3,3,256,256]{3,2,1,0:T(8,128)S(1)} %fusion.161), channel_id=1, source_target_pairs={{0,2},{1,3},{2,0},{3,1},{4,6},{5,7},{6,4},{7,5},{8,10},{9,11},{10,... | collective-permute-start | bytes 7077896 | tf_op jit(solution)/shard_map/ppermute | solution.py:138
  419.0 59.5 %copy-start.20 = (f32[1,3,256,256]{3,2,1,0:T(8,128)}, f32[1,3,256,256]{3,2,1,0:T(8,128)S(1)}, u32[]{:S(2)}) copy-start(f32[1,3,256,256]{3,2,1,0:T(8,128)S(1)} %maximum_bitcast_fusion.2) | copy-start | bytes 2359300
  419.1 59.4 %copy-start.21 = (f32[1,3,256,256]{3,2,1,0:T(8,128)}, f32[1,3,256,256]{3,2,1,0:T(8,128)S(1)}, u32[]{:S(2)}) copy-start(f32[1,3,256,256]{3,2,1,0:T(8,128)S(1)} %maximum_bitcast_fusion.1) | copy-start | bytes 2359300
  423.7 46.7 %copy-start.38 = (f32[3,3,256,256]{3,2,1,0:T(8,128)S(1)}, f32[3,3,256,256]{3,2,1,0:T(8,128)}, u32[]{:S(2)}) copy-start(f32[3,3,256,256]{3,2,1,0:T(8,128)} %copy-done.37) | copy-start | bytes 7077892
  423.8 54.7 %copy-start.22 = (f32[1,3,256,256]{3,2,1,0:T(8,128)}, f32[1,3,256,256]{3,2,1,0:T(8,128)S(1)}, u32[]{:S(2)}) copy-start(f32[1,3,256,256]{3,2,1,0:T(8,128)S(1)} %maximum_bitcast_fusion) | copy-start | bytes 2359300
  425.5 53.0 %collective-permute-start = (f32[3,3,256,256]{3,2,1,0:T(8,128)}, f32[3,3,256,256]{3,2,1,0:T(8,128)}, u32[]{:S(2)}, u32[]{:S(2)}) collective-permute-start(f32[3,3,256,256]{3,2,1,0:T(8,128)} %pad_maximum_fusion.7), channel_id=1, source_target_pairs={{0,1},{1,0},{2,3},{3,2},{4,5},{5,4},{6,7},{7,6},{8,9},{9,8},{10,11... | collective-permute-start | bytes 7077896 | tf_op jit(solution)/shard_map/ppermute | solution.py:138
  472.4 100.8 %reduce-scatter.3.cloned.1.call-start = ((), (), s32[]{:S(2)}) async-start(), calls=%async_computation.6 | async-start | bytes 2654208 | tf_op jit(solution)/shard_map/reduce_scatter | solution.py:141
  480.5 51.9 %collective-permute-start.1 = (f32[3,3,256,256]{3,2,1,0:T(8,128)S(1)}, f32[3,3,256,256]{3,2,1,0:T(8,128)S(1)}, u32[]{:S(2)}, u32[]{:S(2)}) collective-permute-start(f32[3,3,256,256]{3,2,1,0:T(8,128)S(1)} %fusion.162), channel_id=1, source_target_pairs={{0,2},{1,3},{2,0},{3,1},{4,6},{5,7},{6,4},{7,5},{8,10},{9,11},{10,... | collective-permute-start | bytes 7077896 | tf_op jit(solution)/shard_map/ppermute | solution.py:138
  532.5 4.4 copy-start.14
  (28 other events, 74.2 us)
Sparse Core Ops, SparseCore 0:
  12.0 33.5 all-gather.4
  47.2 31.4 all-gather.6
  155.8 30.0 all-gather.8
  339.9 43.2 all-gather.10
  472.5 37.0 reduce-scatter.4
  537.0 36.1 reduce-scatter.2
